TPU v7x, 256 devices: a whole 4x4x8 slice. The times are simulated.
256 devices in a mesh: grp: 2 (over core), seq: 32 (over z, x), head: 4 (over y).
Axes of the slice: x: 4, y: 4, z: 8, core: 2. Of those that a mesh axis runs over, the one named last changes fastest.
Arguments:
- queries: bfloat16 [6144, 64, 128], P('seq', ('grp', 'head')), may hold values from -6 to 6
- keys: bfloat16 [6144, 64, 128], P('seq', ('grp', 'head')), may hold values from -6 to 6
- values: bfloat16 [6144, 64, 128], P('seq', ('grp', 'head')), may hold values from -6 to 6
- documents: int32 [6144], P('seq'), may hold values from 0 to 3, never falling along the last dimension, each value on 1 to 4608 neighbouring positions
- feature_map: float32 [64, 128, 128], P(('grp', 'head')), may hold values from -8 to 8
Outputs:
- teacher_out: bfloat16 [6144, 64, 128], P('seq', ('grp', 'head'))
- student_out: bfloat16 [6144, 64, 128], P('seq', ('grp', 'head'))
- loss: float32 [], replicated
- feature_grad: float32 [64, 128, 128], P(('grp', 'head'))
All inputs are finite; a program needn't handle non-finite values.
Results may differ from a plain program's by a relative error of at most 0.006.
Values may be sent and summed in bfloat16 or wider, within the bound.
A program may use at most 192 MiB of HBM per device.

v0:
```python
import functools
import jax
import jax.numpy as jnp
from jax import lax
from jax.sharding import Mesh
from jax.sharding import PartitionSpec as P

WINDOW = 64
SEQ = ("seq_0", "seq_1")
GRP_SEQ_HEAD = ("grp", "seq_0", "seq_1", "head")
exact_mode = lax.Precision.HIGHEST
masked_value = -1e30


def passed_along(block, axis, distance):
    devices = range(lax.axis_size(axis))
    route = [(i - distance, i) for i in devices if i - distance in devices]
    return lax.ppermute(block, axis, route)


def filled_with(array, identity):
    return jax.tree.map(
        lambda part, zero: jnp.zeros_like(part) + jnp.asarray(zero, part.dtype), array, identity
    )


def carried_in(array, axes, combine, identity, reverse):
    before = start = filled_with(array, identity)
    subtotal = array
    for axis in reversed(axes):
        peers, mine = (lax.axis_size(axis), lax.axis_index(axis))
        pieces = jax.tree.map(lambda part: lax.all_gather(part, axis), subtotal)
        inside, subtotal = (start, start)
        for k in reversed(range(peers)) if reverse else range(peers):
            passed = k > mine if reverse else k < mine
            subtotal = combine(subtotal, jax.tree.map(lambda part: part[k], pieces))
            inside = jax.tree.map(lambda new, old: jnp.where(passed, new, old), subtotal, inside)
        before = combine(inside, before)
    return before


def over_axes(array, axes):
    return functools.reduce(lax.psum, axes, array)


def features(inputs, weights):
    logits = jnp.einsum("rhd,hdf->rhf", inputs, weights, precision=exact_mode)
    return jnp.concatenate(
        [jax.nn.softmax(logits, axis=-1), jax.nn.softmax(-logits, axis=-1)], axis=-1
    )


def join_up(earlier, later):
    merged_tag = jnp.maximum(earlier[0], later[0])
    early_keep = (earlier[0] == merged_tag).astype(earlier[1].dtype)
    late_keep = (later[0] == merged_tag).astype(later[1].dtype)
    return (
        merged_tag,
        early_keep * earlier[1] + late_keep * later[1],
        early_keep * earlier[2] + late_keep * later[2],
    )


def join_down(earlier, later):
    merged_tag = jnp.minimum(earlier[0], later[0])
    early_keep = (earlier[0] == merged_tag).astype(earlier[1].dtype)
    late_keep = (later[0] == merged_tag).astype(later[1].dtype)
    return (
        merged_tag,
        early_keep * earlier[1] + late_keep * later[1],
        early_keep * earlier[2] + late_keep * later[2],
    )


def body(queries, keys, values, documents, feature_map):
    tok_rows, head_count, head_width = queries.shape
    half_feat = feature_map.shape[2] // 2
    score_scale = head_width ** (-0.5)
    seq_place = lax.axis_index(SEQ)
    seq_count = lax.axis_size(SEQ)
    first_row = seq_place * tok_rows
    doc_float = documents.astype(jnp.float32)
    doc_marks = (documents + 1).astype(jnp.bfloat16)
    query_pos = first_row + jnp.arange(tok_rows)
    key_piece = lax.all_gather(keys, SEQ, axis=0, tiled=True)
    value_piece = lax.all_gather(values, SEQ, axis=0, tiled=True)
    mark_piece = lax.all_gather(doc_marks, SEQ, axis=0, tiled=True)
    key_pos = jnp.arange(key_piece.shape[0])
    same_doc = mark_piece.astype(jnp.float32)[None, :] - 1.0 == doc_float[:, None]
    allowed = (same_doc & (key_pos[None, :] <= query_pos[:, None]))[:, None, :]
    scores = (
        jnp.einsum("ihd,jhd->ihj", queries, key_piece, preferred_element_type=jnp.float32)
        * score_scale
    )
    scores = jnp.where(allowed, scores, masked_value)
    row_max = jnp.full((tok_rows, head_count), masked_value, jnp.float32)
    new_max = jnp.maximum(row_max, jnp.max(scores, axis=-1))
    probabilities = jnp.where(allowed, jnp.exp(scores - new_max[:, :, None]), 0.0)
    totals = jnp.sum(probabilities, axis=-1)
    numerator = jnp.einsum(
        "ihj,jhd->ihd",
        probabilities.astype(jnp.bfloat16),
        value_piece,
        preferred_element_type=jnp.float32,
    )
    row_max, totals, numerator = (new_max, totals, numerator)
    teacher_out = (numerator / totals[:, :, None]).astype(jnp.bfloat16)
    target = teacher_out.astype(jnp.float32)
    halo_keys, halo_values, halo_marks = passed_along(
        (keys[tok_rows - WINDOW :], values[tok_rows - WINDOW :], doc_marks[tok_rows - WINDOW :]),
        SEQ,
        1,
    )
    key_joined = jnp.concatenate([halo_keys, keys], axis=0)
    key_float = key_joined.astype(jnp.float32)
    value_float = jnp.concatenate([halo_values, values], axis=0).astype(jnp.float32)
    doc_all = jnp.concatenate([halo_marks.astype(jnp.float32) - 1.0, doc_float], axis=0)
    query_float = queries.astype(jnp.float32)
    distance = jnp.arange(tok_rows)[:, None] + WINDOW - jnp.arange(tok_rows + WINDOW)[None, :]
    same_doc = doc_float[:, None] == doc_all[None, :]
    in_window = same_doc & (distance >= 0) & (distance < WINDOW)
    beyond = same_doc & (distance >= WINDOW)
    scores = (
        jnp.einsum("ihd,jhd->hij", queries, key_joined, preferred_element_type=jnp.float32)
        * score_scale
    )
    window_row = jnp.max(jnp.where(in_window[None], scores, masked_value), axis=-1, keepdims=True)
    window_weight = jnp.where(in_window[None], jnp.exp(scores - window_row), 0.0)
    elem_keys = key_float[:tok_rows]
    elem_values = value_float[:tok_rows]
    elem_docs = doc_all[:tok_rows]
    elem_tag = elem_docs[tok_rows - 1]
    in_tail = (elem_docs == elem_tag).astype(jnp.float32)

    def element(weights):
        masked_feat = features(elem_keys, weights[:, :, half_feat:]) * in_tail[:, None, None]
        return (
            jnp.einsum("jhf,jhd->hfd", masked_feat, elem_values, precision=exact_mode),
            jnp.sum(masked_feat, axis=0),
        )

    (elem_state, elem_norm), element_pullback = jax.vjp(element, feature_map)
    blank_state = jnp.zeros_like(elem_state)
    blank_norm = jnp.zeros_like(elem_norm)
    tag_in, state_in, norm_in = carried_in(
        (elem_tag, elem_state, elem_norm),
        SEQ,
        join_up,
        (jnp.float32(-2.0), blank_state, blank_norm),
        False,
    )
    uses_state = (doc_float == tag_in).astype(jnp.float32)[:, None]
    normaliser = 1.0 / (tok_rows * seq_count * head_count * lax.axis_size(("grp", "head")))

    def local_loss(weights, state, norm):
        query_feat = features(query_float, weights[:, :, :half_feat])
        key_feat = features(key_float, weights[:, :, half_feat:])
        linear = jnp.where(
            beyond[None],
            jnp.einsum("ihf,jhf->hij", query_feat, key_feat, precision=exact_mode),
            0.0,
        )
        weight = window_weight + linear
        numer_sum = jnp.einsum("hij,jhd->ihd", weight, value_float, precision=exact_mode)
        numer_sum = numer_sum + uses_state[:, :, None] * jnp.einsum(
            "ihf,hfd->ihd", query_feat, state, precision=exact_mode
        )
        denominator = jnp.sum(weight, axis=-1).T + uses_state * jnp.einsum(
            "ihf,hf->ih", query_feat, norm, precision=exact_mode
        )
        output = numer_sum / denominator[:, :, None]
        return (jnp.sum(jnp.square(output - target)) * normaliser, output)

    local_part, local_pullback, output = jax.vjp(
        local_loss, feature_map, state_in, norm_in, has_aux=True
    )
    grad_direct, grad_state, grad_norm = local_pullback(jnp.ones_like(local_part))
    back_tag, carried_state, carried_norm = carried_in(
        (tag_in, grad_state, grad_norm),
        SEQ,
        join_down,
        (jnp.float32(1000000000.0), blank_state, blank_norm),
        True,
    )
    total_grad = grad_direct + element_pullback((carried_state, carried_norm))[0]
    feature_grad = over_axes(total_grad, SEQ)
    loss_total = jax.tree.map(lambda part: over_axes(part, GRP_SEQ_HEAD), local_part)
    return (teacher_out, output.astype(jnp.bfloat16), loss_total, feature_grad)


def solution(mesh):
    split = Mesh(
        mesh.devices.reshape(mesh.shape["grp"], 8, 4, mesh.shape["head"]),
        ("grp", "seq_0", "seq_1", "head"),
    )
    return jax.shard_map(
        body,
        mesh=split,
        in_specs=(
            P(SEQ, ("grp", "head"), None),
            P(SEQ, ("grp", "head"), None),
            P(SEQ, ("grp", "head"), None),
            P(SEQ),
            P(("grp", "head"), None, None),
        ),
        out_specs=(
            P(SEQ, ("grp", "head"), None),
            P(SEQ, ("grp", "head"), None),
            P(),
            P(("grp", "head"), None, None),
        ),
        check_vma=False,
    )
```

profile of v0, /device:TPU:8, one launch (start us, length us, event | category | flops | bytes accessed | tf_op | source)
XLA Modules:
  0.0 640.9 jit_solution(11608733308166562102)
XLA Ops:
  7.3 1.1 copy.34
  8.4 3.4 collective-permute-start.2
  12.6 3.4 collective-permute-start.1
  16.0 1.1 copy.36
  17.1 3.1 collective-permute-start
  20.8 1.2 slice_dynamic-update-slice_fusion
  23.0 1.0 convolution_bitcast_fusion.1
  27.2 1.5 fusion.37
  28.8 11.1 %all-reduce.4 = f32[4]{0:T(128)S(1)} all-reduce(f32[4]{0:T(128)S(1)} %get-tuple-element.28), channel_id=1, replica_groups=mesh['grp'=2,'seq_0'=8,'seq_1'=4,'head'=4] {'seq_1'}, use_global_device_ids=true, to_apply=%add.4 | all-reduce | flops 4 | bytes 32
  45.8 18.7 %all-gather.19.cloned.1.call-done = f32[32,128,128]{2,1,0:T(8,128)} async-done(((f32[8,128,128]{2,1,0:T(8,128)}), f32[32,128,128]{2,1,0:T(8,128)}) %all-gather.19.cloned.1.call-update) | async-done | bytes 2097168 | tf_op jit(solution)/shard_map/all_gather | solution.py:32
  64.5 2.5 fusion.75
  69.8 17.9 %all-reduce.5 = f32[8]{0:T(128)S(1)} all-reduce(f32[8]{0:T(128)S(1)} %dynamic-update-slice.2), channel_id=1, replica_groups=mesh['grp'=2,'seq_0'=8,'seq_1'=4,'head'=4] {'seq_0'}, use_global_device_ids=true, to_apply=%add.5 | all-reduce | flops 8 | bytes 64
  100.3 142.1 %all-reduce.3 = bf16[6144]{0:T(1024)(128)(2,1)S(1)} all-reduce(bf16[6144]{0:T(1024)(128)(2,1)S(1)} %dynamic-update-slice), channel_id=1, replica_groups=mesh['grp'=2,'seq_0'=8,'seq_1'=4,'head'=4] {'seq_0','seq_1'}, use_global_device_ids=true, to_apply=%add.3 | all-reduce | flops 6144 | bytes 24576
  243.3 0.9 fusion.273
  246.1 1.0 fusion.13
  247.6 12.0 %all-gather.1 = f32[32,128]{1,0:T(8,128)S(1)} all-gather(f32[8,128]{1,0:T(8,128)S(1)} %fusion.36), channel_id=3, replica_groups=mesh['grp'=2,'seq_0'=8,'seq_1'=4,'head'=4] {'seq_1'}, dimensions={0}, use_global_device_ids=true | all-gather | bytes 20480 | tf_op jit(solution)/shard_map/all_gather | solution.py:32
  259.6 25.2 %all_gather.81 = f32[8,8,128]{2,1,0:T(8,128)S(1)} all-gather(f32[1,8,128]{2,1,0:T(8,128)S(1)} %fusion.245), channel_id=1, replica_groups=mesh['grp'=2,'seq_0'=8,'seq_1'=4,'head'=4] {'seq_0'}, dimensions={0}, use_global_device_ids=true | all-gather | bytes 36864 | tf_op jit(solution)/shard_map/all_gather | solution.py:32
  284.8 0.9 convolution_bitcast_fusion.2
  288.4 2.0 fusion.35
  291.5 2.0 fusion.277
  293.5 4.0 fusion.67
  298.3 2.7 convolution_multiply_fusion.1
  301.1 18.7 %fusion.7 = (f32[192,8]{0,1:T(8,128)S(1)}, f32[8,6144,192]{1,2,0:T(8,128)}) fusion(pred[192,6144]{1,0:T(8,128)(4,1)S(1)} %fusion.13, bf16[6144,8,128]{2,0,1:T(8,128)(2,1)} %all-gather.11.cloned.1.call-done, bf16[192,8,128]{2,1,0:T(8,128)(2,1)S(1)} %copy-done), kind=kOutput, calls=%fused_computation.9 | convolution fusion | flops 2444229120 | bytes 51910656 | tf_op jit(solution)/shard_map/ihd,jhd->ihj/dot_general | solution.py:92
  319.7 18.9 %fusion.8 = f32[192,8]{0,1:T(8,128)S(1)} fusion(f32[8,6144,192]{1,2,0:T(8,128)} %get-tuple-element.71, f32[192,8]{0,1:T(8,128)S(1)} %broadcast_maximum_fusion, pred[192,6144]{1,0:T(8,128)(4,1)S(1)} %fusion.13), kind=kLoop, calls=%fused_computation.10 | loop fusion | flops 47184384 | bytes 38940672 | tf_op jit(solution)/shard_map/reduce_sum | solution.py:99
  338.6 24.1 %all-gather.13.cloned.1.call-done = bf16[6144,8,128]{2,0,1:T(8,128)(2,1)} async-done(((bf16[192,8,128]{2,0,1:T(8,128)(2,1)}), bf16[6144,8,128]{2,0,1:T(8,128)(2,1)}) %all-gather.13.cloned.1.call-update) | async-done | bytes 12582928 | tf_op jit(solution)/shard_map/all_gather | solution.py:86
  362.8 21.5 %fusion.10 = f32[8,192,128]{2,1,0:T(8,128)} fusion(bf16[6144,8,128]{2,0,1:T(8,128)(2,1)} %all-gather.13.cloned.1.call-done, f32[8,6144,192]{1,2,0:T(8,128)} %get-tuple-element.71, f32[192,8]{0,1:T(8,128)S(1)} %broadcast_maximum_fusion, pred[192,6144]{1,0:T(8,128)(4,1)S(1)} %fusion.13), kind=kOutput, calls=%fused_computation.12 | convolution fusion | flops 2463105024 | bytes 52303872 | tf_op jit(solution)/shard_map/ihj,jhd->ihd/dot_general | solution.py:100
  384.3 3.7 fusion.40
  388.5 2.0 fusion.44
  391.4 8.6 %all-reduce.6 = f32[4]{0:T(128)S(1)} all-reduce(f32[4]{0:T(128)S(1)} %dynamic-update-slice.3), channel_id=1, replica_groups=mesh['grp'=2,'seq_0'=8,'seq_1'=4,'head'=4] {'seq_1'}, use_global_device_ids=true, to_apply=%add.6 | all-reduce | flops 4 | bytes 32
  405.4 15.7 %all-gather.21.cloned.1.call-done = f32[32,128,128]{2,1,0:T(8,128)} async-done(((f32[8,128,128]{2,1,0:T(8,128)}), f32[32,128,128]{2,1,0:T(8,128)}) %all-gather.21.cloned.1.call-update) | async-done | bytes 2097168 | tf_op jit(solution)/shard_map/all_gather | solution.py:32
  421.1 2.5 fusion.60
  425.8 3.0 psum.42
  428.7 18.6 %all-reduce.8 = (f32[]{:T(128)}, f32[8]{0:T(128)S(1)}) all-reduce(f32[]{:T(128)} %psum.42, f32[8]{0:T(128)S(1)} %dynamic-update-slice.4), channel_id=1, replica_groups=mesh['grp'=2,'seq_0'=8,'seq_1'=4,'head'=4] {'seq_0'}, use_global_device_ids=true, to_apply=%region_19.20 | all-reduce | flops 9 | bytes 72 | tf_op jit(solution)/shard_map/psum | solution.py:43
  457.9 2.0 add_select_fusion
  460.0 1.9 fusion.34
  461.9 1.8 fusion.21
  464.0 1.3 convolution_bitcast_fusion
  465.6 0.9 fusion.213
  466.5 12.0 %all-gather.2 = f32[32,128]{1,0:T(8,128)S(1)} all-gather(f32[8,128]{1,0:T(8,128)S(1)} %bitcast.225), channel_id=4, replica_groups=mesh['grp'=2,'seq_0'=8,'seq_1'=4,'head'=4] {'seq_1'}, dimensions={0}, use_global_device_ids=true | all-gather | bytes 20480 | tf_op jit(solution)/shard_map/all_gather | solution.py:32
  478.5 24.7 %all_gather.88 = f32[8,8,128]{2,1,0:T(8,128)S(1)} all-gather(f32[1,8,128]{2,1,0:T(8,128)S(1)} %fusion.230), channel_id=1, replica_groups=mesh['grp'=2,'seq_0'=8,'seq_1'=4,'head'=4] {'seq_0'}, dimensions={0}, use_global_device_ids=true | all-gather | bytes 36864 | tf_op jit(solution)/shard_map/all_gather | solution.py:32
  505.7 4.1 fusion.19
  511.7 71.1 %all-reduce.12.cloned.1.call-done = f32[8,128,128]{1,2,0:T(8,128)} async-done(((f32[8,128,128]{1,2,0:T(8,128)}), f32[8,128,128]{1,2,0:T(8,128)}) %all-reduce.12.cloned.1.call-update) | async-done | bytes 524304 | tf_op jit(solution)/shard_map/psum | solution.py:43
  582.9 11.1 %psum.44 = f32[]{:T(128)} all-reduce(f32[]{:T(128)} %get-tuple-element.20), channel_id=1, replica_groups=mesh['grp'=2,'seq_0'=8,'seq_1'=4,'head'=4] {'seq_1'}, use_global_device_ids=true, to_apply=%region_20.21 | all-reduce | flops 1 | bytes 8 | tf_op jit(solution)/shard_map/psum | solution.py:43
  593.9 9.2 %psum.45 = f32[]{:T(128)} all-reduce(f32[]{:T(128)} %psum.44), channel_id=1, replica_groups=mesh['grp'=2,'seq_0'=8,'seq_1'=4,'head'=4] {'head'}, use_global_device_ids=true, to_apply=%region_21.22 | all-reduce | flops 1 | bytes 8 | tf_op jit(solution)/shard_map/psum | solution.py:43
  603.2 1.0 copy.56
  604.2 1.0 copy.57
  605.2 26.6 %all-reduce.14.cloned.1.call-done = f32[8,128,128]{1,2,0:T(8,128)} async-done(((f32[8,128,128]{1,2,0:T(8,128)}), f32[8,128,128]{1,2,0:T(8,128)}) %all-reduce.14.cloned.1.call-update) | async-done | bytes 524304 | tf_op jit(solution)/shard_map/psum | solution.py:43
  631.8 2.0 copy.58
  (200 shorter events, 26.8 us)
Async XLA Ops:
  7.2 235.3 %copy-start = (bf16[192,8,128]{2,1,0:T(8,128)(2,1)S(1)}, bf16[192,8,128]{2,1,0:T(8,128)(2,1)}, u32[]{:S(2)}) copy-start(bf16[192,8,128]{2,1,0:T(8,128)(2,1)} %param.5) | copy-start | bytes 1179652
  7.2 13.0 %copy-start.53 = (u32[256]{0:T(256)S(1)}, u32[256]{0:T(256)}, u32[]{:S(2)}) copy-start(u32[256]{0:T(256)} %constant.93) | copy-start | bytes 3076
  7.2 15.7 %copy-start.31 = (bf16[192,8,128]{2,1,0:T(8,128)(2,1)S(1)}, bf16[192,8,128]{2,1,0:T(8,128)(2,1)}, u32[]{:S(2)}) copy-start(bf16[192,8,128]{2,1,0:T(8,128)(2,1)} %param.6) | copy-start | bytes 1179652
  7.2 15.8 %copy-start.11 = (f32[8,128,128]{2,1,0:T(8,128)S(1)}, f32[8,128,128]{2,1,0:T(8,128)}, u32[]{:S(2)}) copy-start(f32[8,128,128]{2,1,0:T(8,128)} %param.9) | copy-start | bytes 1572868
  7.2 57.3 %all-gather.19.cloned.1.call-start = ((), (), s32[]{:S(2)}) async-start(), calls=%async_computation.6 | async-start | bytes 2621440 | tf_op jit(solution)/shard_map/all_gather | solution.py:32
  8.4 16.6 %copy-start.25 = (bf16[192,8,128]{2,0,1:T(8,128)(2,1)}, bf16[192,8,128]{2,0,1:T(8,128)(2,1)S(1)}, u32[]{:S(2)}) copy-start(bf16[192,8,128]{2,0,1:T(8,128)(2,1)S(1)} %copy.34) | copy-start | bytes 1179652
  8.4 14.4 %collective-permute-start.2 = (bf16[64,8,128]{2,0,1:T(8,128)(2,1)S(1)}, bf16[64,8,128]{2,0,1:T(8,128)(2,1)S(1)}, u32[]{:S(2)}, u32[]{:S(2)}) collective-permute-start(bf16[64,8,128]{2,0,1:T(8,128)(2,1)S(1)} %slice.344), channel_id=1, source_target_pairs={{0,4},{4,8},{8,12},{12,16},{16,20},{20,24},{24,28},{28,32},{32,36}... | collective-permute-start | bytes 393224 | tf_op jit(solution)/shard_map/ppermute | solution.py:18
  12.6 10.2 %copy-start.44 = (f32[192]{0:T(256)}, f32[192]{0:T(256)S(1)}, u32[]{:S(2)}) copy-start(f32[192]{0:T(256)S(1)} %get-tuple-element.31) | copy-start | bytes 2308
  12.6 9.5 %collective-permute-start.1 = (bf16[64]{0:T(256)(128)(2,1)S(1)}, bf16[64]{0:T(256)(128)(2,1)S(1)}, u32[]{:S(2)}, u32[]{:S(2)}) collective-permute-start(bf16[64]{0:T(256)(128)(2,1)S(1)} %slice.247), channel_id=1, source_target_pairs={{0,4},{4,8},{8,12},{12,16},{16,20},{20,24},{24,28},{28,32},{32,36}... | collective-permute-start | bytes 392 | tf_op jit(solution)/shard_map/ppermute | solution.py:18
  17.1 8.8 %copy-start.26 = (bf16[192,8,128]{2,0,1:T(8,128)(2,1)}, bf16[192,8,128]{2,0,1:T(8,128)(2,1)S(1)}, u32[]{:S(2)}) copy-start(bf16[192,8,128]{2,0,1:T(8,128)(2,1)S(1)} %copy.36) | copy-start | bytes 1179652
  17.1 8.8 %collective-permute-start = (bf16[64,8,128]{2,0,1:T(8,128)(2,1)S(1)}, bf16[64,8,128]{2,0,1:T(8,128)(2,1)S(1)}, u32[]{:S(2)}, u32[]{:S(2)}) collective-permute-start(bf16[64,8,128]{2,0,1:T(8,128)(2,1)S(1)} %slice.343), channel_id=1, source_target_pairs={{0,4},{4,8},{8,12},{12,16},{16,20},{20,24},{24,28},{28,32},{32,36}... | collective-permute-start | bytes 393224 | tf_op jit(solution)/shard_map/ppermute | solution.py:18
  22.8 3.9 copy-start.46
  23.0 2.9 copy-start.32
  28.7 39.7 %copy-start.52 = (u32[256]{0:T(256)S(1)}, u32[256]{0:T(256)}, u32[]{:S(2)}) copy-start(u32[256]{0:T(256)} %constant.98) | copy-start | bytes 3076
  28.7 264.8 %all-gather.15.cloned.1.call-start = ((), (), s32[]{:S(2)}) async-start(), calls=%async_computation.2 | async-start | bytes 4718592 | tf_op jit(solution)/shard_map/all_gather | solution.py:32
  40.6 58.2 %copy-start.51 = (u32[256]{0:T(256)S(1)}, u32[256]{0:T(256)}, u32[]{:S(2)}) copy-start(u32[256]{0:T(256)} %constant.88) | copy-start | bytes 3076
  45.8 196.6 %copy-start.50 = (s32[192]{0:T(256)S(1)}, s32[192]{0:T(256)}, u32[]{:S(2)}) copy-start(s32[192]{0:T(256)} %param.8) | copy-start | bytes 2308
  67.0 234.1 %all-gather.11.cloned.1.call-start = ((), (), s32[]{:S(2)}) async-start(), calls=%async_computation | async-start | bytes 12976128 | tf_op jit(solution)/shard_map/all_gather | solution.py:85
  67.8 295.0 %all-gather.13.cloned.1.call-start = ((), (), s32[]{:S(2)}) async-start(), calls=%async_computation.1 | async-start | bytes 12976128 | tf_op jit(solution)/shard_map/all_gather | solution.py:86
  68.3 352.8 %all-gather.21.cloned.1.call-start = ((), (), s32[]{:S(2)}) async-start(), calls=%async_computation.7 | async-start | bytes 2621440 | tf_op jit(solution)/shard_map/all_gather | solution.py:32
  243.3 2.8 copy-start.45
  244.3 2.9 copy-start.49
  244.3 3.1 copy-start.8
  244.3 3.1 copy-start.10
  244.3 3.1 copy-start.47
  246.0 38.8 %copy-start.12 = (f32[8,128,128]{2,1,0:T(8,128)S(1)}, f32[8,128,128]{2,1,0:T(8,128)}, u32[]{:S(2)}) copy-start(f32[8,128,128]{2,1,0:T(8,128)} %param.9) | copy-start | bytes 1572868
  286.6 142.1 %copy-start.38 = (f32[256,8]{0,1:T(8,128)}, f32[256,8]{0,1:T(8,128)S(1)}, u32[]{:S(2)}) copy-start(f32[256,8]{0,1:T(8,128)S(1)} %get-tuple-element.64) | copy-start | bytes 24580
  287.5 141.2 %copy-start.40 = (f32[256,8]{0,1:T(8,128)}, f32[256,8]{0,1:T(8,128)S(1)}, u32[]{:S(2)}) copy-start(f32[256,8]{0,1:T(8,128)S(1)} %get-tuple-element.66) | copy-start | bytes 24580
  287.6 2.8 copy-start.1
  287.7 2.8 copy-start.3
  362.8 21.5 %copy-start.28 = (bf16[256,8,128]{2,0,1:T(8,128)(2,1)S(1)}, bf16[256,8,128]{2,0,1:T(8,128)(2,1)}, u32[]{:S(2)}) copy-start(bf16[256,8,128]{2,0,1:T(8,128)(2,1)} %copy-done.27) | copy-start | bytes 1572868
  362.8 21.5 %copy-start.33 = (f32[8,192,256]{2,1,0:T(8,128)S(1)}, f32[8,192,256]{2,1,0:T(8,128)}, u32[]{:S(2)}) copy-start(f32[8,192,256]{2,1,0:T(8,128)} %get-tuple-element.69) | copy-start | bytes 4718596
  362.8 21.5 %copy-start.34 = (f32[8,128,192]{1,2,0:T(8,128)S(1)}, f32[8,128,192]{1,2,0:T(8,128)}, u32[]{:S(2)}) copy-start(f32[8,128,192]{1,2,0:T(8,128)} %convolution_multiply_fusion.1) | copy-start | bytes 2359300
  384.3 3.7 copy-start.35
  390.5 114.6 %all-gather.17.cloned.1.call-start = ((), (), s32[]{:S(2)}) async-start(), calls=%async_computation.3 | async-start | bytes 4718592 | tf_op jit(solution)/shard_map/all_gather | solution.py:32
  423.6 36.3 %copy-start.2 = (f32[256,8,64]{0,2,1:T(8,128)S(1)}, f32[256,8,64]{0,2,1:T(8,128)}, u32[]{:S(2)}) copy-start(f32[256,8,64]{0,2,1:T(8,128)} %copy-done.1) | copy-start | bytes 1572868
  423.6 159.2 %all-reduce.12.cloned.1.call-start = ((), (), s32[]{:S(2)}) async-start(), calls=%async_computation.4 | async-start | bytes 1048576 | tf_op jit(solution)/shard_map/psum | solution.py:43
  457.9 2.0 copy-start.4
  459.9 1.9 copy-start.6
  461.9 1.8 copy-start.18
  461.9 1.8 copy-start.20
  505.1 4.8 copy-start.14
  505.1 4.8 copy-start.16
  505.7 4.2 copy-start.42
  505.7 4.2 copy-start.43
  510.8 92.4 %copy-start.37 = (bf16[192,8,128]{2,0,1:T(8,128)(2,1)S(1)}, bf16[192,8,128]{2,0,1:T(8,128)(2,1)}, u32[]{:S(2)}) copy-start(bf16[192,8,128]{2,0,1:T(8,128)(2,1)} %get-tuple-element.22) | copy-start | bytes 1179652
  510.8 93.4 %copy-start.36 = (bf16[192,8,128]{2,0,1:T(8,128)(2,1)S(1)}, bf16[192,8,128]{2,0,1:T(8,128)(2,1)}, u32[]{:S(2)}) copy-start(bf16[192,8,128]{2,0,1:T(8,128)(2,1)} %get-tuple-element.25) | copy-start | bytes 1179652
  511.7 120.1 %all-reduce.14.cloned.1.call-start = ((), (), s32[]{:S(2)}) async-start(), calls=%async_computation.5 | async-start | bytes 1048576 | tf_op jit(solution)/shard_map/psum | solution.py:43
  (17 other events, 16.2 us)
Sparse Core Ops, SparseCore 0:
  28.8 35.6 all-gather.18
  67.1 54.9 all-gather.14
  125.3 118.4 all-gather.10
  246.8 115.8 all-gather.12
  390.7 30.3 all-gather.20
  423.7 55.0 all-gather.16
  511.8 71.0 all-reduce.11
  585.2 46.5 all-reduce.13
where the time goes:
time: 647 us; the launch traced here: 641 us
  blocking collectives  295 us (46%)
  waiting for transfers between devices  158 us (24%)
  matrix products  69.9 us (11%)
  between operations  47.1 us (7%)
  other arithmetic  41.8 us (6%)
  local copies, waits for them, and re-layouts  18.9 us (3%)
  starting transfers between devices  10.2 us (2%)
    unnamed x4, blocking collectives  180 us
    psum x2, waiting for transfers between devices, over_axes(): return functools.reduce(lax.psum, axes, array)  97.7 us
    all_gather x4, blocking collectives, carried_in(): pieces = jax.tree.map(lambda part: lax.all_gather(part, axis), subtotal)  73.9 us
    psum x4, blocking collectives, over_axes(): return functools.reduce(lax.psum, axes, array)  41.8 us
    all_gather x4, waiting for transfers between devices, carried_in(): pieces = jax.tree.map(lambda part: lax.all_gather(part, axis), subtotal)  34.4 us
    all_gather x1, waiting for transfers between devices, body(): value_piece = lax.all_gather(values, SEQ, axis=0, tiled=True)  24.1 us
    dot_general x1, matrix products, body(): jnp.einsum('ihj,jhd->ihd', probabilities.astype(jnp.bfloat16), value_piec...  21.5 us
    reduce_sum x1, other arithmetic, body(): totals = jnp.sum(probabilities, axis=-1)  18.9 us
  transfers between devices with their start and end apart: 11, of which 5 were waited for; matrix products, arithmetic and copies ran while one was open for 13% of the time, Pallas kernels for 0%

commit v1 on v0

--- a/solution.py
+++ b/solution.py
@@ -83,7 +83,14 @@
     doc_marks = (documents + 1).astype(jnp.bfloat16)
     query_pos = first_row + jnp.arange(tok_rows)
     key_piece = lax.all_gather(keys, SEQ, axis=0, tiled=True)
-    value_piece = lax.all_gather(values, SEQ, axis=0, tiled=True)
+
+    def paths_cut(xs):
+        last = lax.axis_size(SEQ)
+        z1 = jnp.stack(last * [xs], axis=0)
+        small = lax.all_to_all(z1, axis_name=SEQ, split_axis=0, concat_axis=0)
+        return jnp.concatenate(small, axis=0)
+
+    value_piece = paths_cut(values)
     mark_piece = lax.all_gather(doc_marks, SEQ, axis=0, tiled=True)
     key_pos = jnp.arange(key_piece.shape[0])
     same_doc = mark_piece.astype(jnp.float32)[None, :] - 1.0 == doc_float[:, None]

time: 647 us -> 1020 us (1.58)
  blocking collectives: 295 us -> 656 us
  waiting for transfers between devices: 158 us -> 135 us
  local copies, waits for them, and re-layouts: 18.9 us -> 39.6 us
    unnamed x4, blocking collectives: 180 us -> 538 us
    all_gather x1 -> x0, waiting for transfers between devices: 24.1 us -> none  [body(): value_piece = lax.all_gather(values, SEQ, axis=0, tiled=True)]
    all_to_all x0 -> x1, local copies, waits for them, and re-layouts: none -> 11.8 us  [paths_cut(): small = lax.all_to_all(z1, axis_name=SEQ, split_axis=0, concat_axis=0)]
  transfers between devices with their start and end apart: 11 -> 11, of which waited for: 5 -> 4; matrix products, arithmetic and copies ran while one was open for 13% -> 9% of each run, Pallas kernels for 0% -> 0%
where the time goes in v1:
time: 1020 us; the launch traced here: 1010 us
  blocking collectives  656 us (64%)
  waiting for transfers between devices  135 us (13%)
  matrix products  74.4 us (7%)
  between operations  47 us (5%)
  other arithmetic  41.1 us (4%)
  local copies, waits for them, and re-layouts  39.6 us (4%)
  starting transfers between devices  19 us (2%)
    unnamed x4, blocking collectives  538 us
    psum x2, waiting for transfers between devices, over_axes(): return functools.reduce(lax.psum, axes, array)  97.7 us
    all_gather x4, blocking collectives, carried_in(): pieces = jax.tree.map(lambda part: lax.all_gather(part, axis), subtotal)  76.1 us
    psum x4, blocking collectives, over_axes(): return functools.reduce(lax.psum, axes, array)  41.9 us
    all_gather x4, waiting for transfers between devices, carried_in(): pieces = jax.tree.map(lambda part: lax.all_gather(part, axis), subtotal)  36.7 us
    dot_general x1, matrix products, body(): jnp.einsum('ihj,jhd->ihd', probabilities.astype(jnp.bfloat16), value_piec...  21.5 us
  transfers between devices with their start and end apart: 11, of which 4 were waited for; matrix products, arithmetic and copies ran while one was open for 9% of the time, Pallas kernels for 0%

profile of v1, /device:TPU:8, one launch (start us, length us, event | category | flops | bytes accessed | tf_op | source)
XLA Modules:
  0.0 1012.4 jit_solution(4221319601365643182)
XLA Ops:
  7.2 1.1 copy.34
  8.4 3.4 collective-permute-start.2
  12.6 3.4 collective-permute-start.1
  17.1 3.1 collective-permute-start
  20.2 1.3 dynamic-slice.1
  21.5 1.2 slice_dynamic-update-slice_fusion
  23.5 1.1 constant_dynamic-update-slice_fusion.2
  24.6 2.1 convolution_bitcast_fusion.1
  30.3 1.5 fusion.37
  31.9 11.1 %all-reduce.4 = f32[4]{0:T(128)S(1)} all-reduce(f32[4]{0:T(128)S(1)} %get-tuple-element.28), channel_id=1, replica_groups=mesh['grp'=2,'seq_0'=8,'seq_1'=4,'head'=4] {'seq_1'}, use_global_device_ids=true, to_apply=%add.4 | all-reduce | flops 4 | bytes 32
  48.7 19.0 %all-gather.16.cloned.1.call-done = f32[32,128,128]{2,1,0:T(8,128)} async-done(((f32[8,128,128]{2,1,0:T(8,128)}), f32[32,128,128]{2,1,0:T(8,128)}) %all-gather.16.cloned.1.call-update) | async-done | bytes 2097168 | tf_op jit(solution)/shard_map/all_gather | solution.py:32
  67.7 2.5 fusion.75
  70.9 7.7 stack.2
  78.6 8.8 all-to-all-start
  88.8 381.6 %all-reduce.5 = f32[8]{0:T(128)S(1)} all-reduce(f32[8]{0:T(128)S(1)} %dynamic-update-slice.2), channel_id=1, replica_groups=mesh['grp'=2,'seq_0'=8,'seq_1'=4,'head'=4] {'seq_0'}, use_global_device_ids=true, to_apply=%add.5 | all-reduce | flops 8 | bytes 64
  482.5 137.7 %all-reduce.3 = bf16[6144]{0:T(1024)(128)(2,1)S(1)} all-reduce(bf16[6144]{0:T(1024)(128)(2,1)S(1)} %dynamic-update-slice), channel_id=1, replica_groups=mesh['grp'=2,'seq_0'=8,'seq_1'=4,'head'=4] {'seq_0','seq_1'}, use_global_device_ids=true, to_apply=%add.3 | all-reduce | flops 6144 | bytes 24576
  625.1 1.4 fusion.36
  626.6 12.0 %all-gather.1 = f32[32,128]{1,0:T(8,128)S(1)} all-gather(f32[8,128]{1,0:T(8,128)S(1)} %fusion.36), channel_id=3, replica_groups=mesh['grp'=2,'seq_0'=8,'seq_1'=4,'head'=4] {'seq_1'}, dimensions={0}, use_global_device_ids=true | all-gather | bytes 20480 | tf_op jit(solution)/shard_map/all_gather | solution.py:32
  638.6 27.4 %all_gather.77 = f32[8,8,128]{2,1,0:T(8,128)S(1)} all-gather(f32[1,8,128]{2,1,0:T(8,128)S(1)} %fusion.245), channel_id=1, replica_groups=mesh['grp'=2,'seq_0'=8,'seq_1'=4,'head'=4] {'seq_0'}, dimensions={0}, use_global_device_ids=true | all-gather | bytes 36864 | tf_op jit(solution)/shard_map/all_gather | solution.py:32
  666.0 2.0 convolution_bitcast_fusion.2
  670.5 2.0 fusion.35
  673.7 2.0 fusion.277
  675.7 3.7 fusion.67
  680.2 2.7 convolution_multiply_fusion.1
  682.9 18.0 %fusion.7 = (f32[192,8]{0,1:T(8,128)S(1)}, f32[8,6144,192]{1,2,0:T(8,128)}) fusion(pred[192,6144]{1,0:T(8,128)(4,1)S(1)} %fusion.13, bf16[6144,8,128]{2,0,1:T(8,128)(2,1)} %all-gather.10.cloned.1.call-done, bf16[192,8,128]{2,1,0:T(8,128)(2,1)S(1)} %copy-done), kind=kOutput, calls=%fused_computation.9 | convolution fusion | flops 2444229120 | bytes 51910656 | tf_op jit(solution)/shard_map/ihd,jhd->ihj/dot_general | solution.py:99
  700.9 18.6 %fusion.8 = f32[192,8]{0,1:T(8,128)S(1)} fusion(f32[8,6144,192]{1,2,0:T(8,128)} %get-tuple-element.71, f32[192,8]{0,1:T(8,128)S(1)} %broadcast_maximum_fusion, pred[192,6144]{1,0:T(8,128)(4,1)S(1)} %fusion.13), kind=kLoop, calls=%fused_computation.10 | loop fusion | flops 47184384 | bytes 38940672 | tf_op jit(solution)/shard_map/reduce_sum | solution.py:106
  719.5 11.8 %copy.37 = bf16[32,192,8,128]{3,1,0,2:T(8,128)(2,1)} copy(bf16[32,192,8,128]{3,1,2,0:T(8,128)(2,1)} %all-to-all-done) | data formatting | bytes 25165824 | tf_op jit(solution)/shard_map/all_to_all | solution.py:90
  731.3 21.5 %fusion.10 = f32[8,192,128]{2,1,0:T(8,128)} fusion(bf16[6144,8,128]{2,0,1:T(8,128)(2,1)} %bitcast.223, f32[8,6144,192]{1,2,0:T(8,128)} %get-tuple-element.71, f32[192,8]{0,1:T(8,128)S(1)} %broadcast_maximum_fusion, pred[192,6144]{1,0:T(8,128)(4,1)S(1)} %fusion.13), kind=kOutput, calls=%fused_computation.12 | convolution fusion | flops 2463105024 | bytes 52303872 | tf_op jit(solution)/shard_map/ihj,jhd->ihd/dot_general | solution.py:107
  752.9 3.7 fusion.40
  757.1 2.0 fusion.44
  759.9 7.7 all-reduce.6
  773.4 17.7 %all-gather.18.cloned.1.call-done = f32[32,128,128]{2,1,0:T(8,128)} async-done(((f32[8,128,128]{2,1,0:T(8,128)}), f32[32,128,128]{2,1,0:T(8,128)}) %all-gather.18.cloned.1.call-update) | async-done | bytes 2097168 | tf_op jit(solution)/shard_map/all_gather | solution.py:32
  791.1 2.5 fusion.60
  795.0 3.0 psum.42
  798.0 18.6 %all-reduce.8 = (f32[]{:T(128)}, f32[8]{0:T(128)S(1)}) all-reduce(f32[]{:T(128)} %psum.42, f32[8]{0:T(128)S(1)} %dynamic-update-slice.4), channel_id=1, replica_groups=mesh['grp'=2,'seq_0'=8,'seq_1'=4,'head'=4] {'seq_0'}, use_global_device_ids=true, to_apply=%region_19.20 | all-reduce | flops 9 | bytes 72 | tf_op jit(solution)/shard_map/psum | solution.py:43
  827.7 1.9 add_select_fusion
  829.7 3.1 fusion.34
  832.8 2.9 fusion.21
  836.0 1.3 convolution_bitcast_fusion
  838.5 12.0 %all-gather.2 = f32[32,128]{1,0:T(8,128)S(1)} all-gather(f32[8,128]{1,0:T(8,128)S(1)} %bitcast.227), channel_id=4, replica_groups=mesh['grp'=2,'seq_0'=8,'seq_1'=4,'head'=4] {'seq_1'}, dimensions={0}, use_global_device_ids=true | all-gather | bytes 20480 | tf_op jit(solution)/shard_map/all_gather | solution.py:32
  850.6 24.7 %all_gather.84 = f32[8,8,128]{2,1,0:T(8,128)S(1)} all-gather(f32[1,8,128]{2,1,0:T(8,128)S(1)} %fusion.230), channel_id=1, replica_groups=mesh['grp'=2,'seq_0'=8,'seq_1'=4,'head'=4] {'seq_0'}, dimensions={0}, use_global_device_ids=true | all-gather | bytes 36864 | tf_op jit(solution)/shard_map/all_gather | solution.py:32
  876.0 1.3 fusion.85
  877.3 4.2 fusion.19
  883.3 71.1 %all-reduce.12.cloned.1.call-done = f32[8,128,128]{1,2,0:T(8,128)} async-done(((f32[8,128,128]{1,2,0:T(8,128)}), f32[8,128,128]{1,2,0:T(8,128)}) %all-reduce.12.cloned.1.call-update) | async-done | bytes 524304 | tf_op jit(solution)/shard_map/psum | solution.py:43
  954.5 11.1 %psum.44 = f32[]{:T(128)} all-reduce(f32[]{:T(128)} %get-tuple-element.20), channel_id=1, replica_groups=mesh['grp'=2,'seq_0'=8,'seq_1'=4,'head'=4] {'seq_1'}, use_global_device_ids=true, to_apply=%region_20.21 | all-reduce | flops 1 | bytes 8 | tf_op jit(solution)/shard_map/psum | solution.py:43
  965.5 9.2 psum.45
  976.8 26.5 %all-reduce.14.cloned.1.call-done = f32[8,128,128]{1,2,0:T(8,128)} async-done(((f32[8,128,128]{1,2,0:T(8,128)}), f32[8,128,128]{1,2,0:T(8,128)}) %all-reduce.14.cloned.1.call-update) | async-done | bytes 524304 | tf_op jit(solution)/shard_map/psum | solution.py:43
  1003.3 2.0 copy.59
  (173 shorter events, 29.0 us)
Async XLA Ops:
  7.2 613.1 %copy-start = (bf16[192,8,128]{2,1,0:T(8,128)(2,1)S(1)}, bf16[192,8,128]{2,1,0:T(8,128)(2,1)}, u32[]{:S(2)}) copy-start(bf16[192,8,128]{2,1,0:T(8,128)(2,1)} %param.5) | copy-start | bytes 1179652
  7.2 21.4 %copy-start.24 = (bf16[192,8,128]{2,1,0:T(8,128)(2,1)S(1)}, bf16[192,8,128]{2,1,0:T(8,128)(2,1)}, u32[]{:S(2)}) copy-start(bf16[192,8,128]{2,1,0:T(8,128)(2,1)} %param.7) | copy-start | bytes 1179652
  7.2 60.5 %all-gather.16.cloned.1.call-start = ((), (), s32[]{:S(2)}) async-start(), calls=%async_computation.6 | async-start | bytes 2621440 | tf_op jit(solution)/shard_map/all_gather | solution.py:32
  8.4 20.4 %copy-start.19 = (bf16[192,8,128]{2,0,1:T(8,128)(2,1)}, bf16[192,8,128]{2,0,1:T(8,128)(2,1)S(1)}, u32[]{:S(2)}) copy-start(bf16[192,8,128]{2,0,1:T(8,128)(2,1)S(1)} %copy.34) | copy-start | bytes 1179652
  8.4 15.0 %collective-permute-start.2 = (bf16[64,8,128]{2,0,1:T(8,128)(2,1)S(1)}, bf16[64,8,128]{2,0,1:T(8,128)(2,1)S(1)}, u32[]{:S(2)}, u32[]{:S(2)}) collective-permute-start(bf16[64,8,128]{2,0,1:T(8,128)(2,1)S(1)} %slice.344), channel_id=1, source_target_pairs={{0,4},{4,8},{8,12},{12,16},{16,20},{20,24},{24,28},{28,32},{32,36}... | collective-permute-start | bytes 393224 | tf_op jit(solution)/shard_map/ppermute | solution.py:18
  12.6 15.9 %copy-start.31 = (f32[192]{0:T(256)}, f32[192]{0:T(256)S(1)}, u32[]{:S(2)}) copy-start(f32[192]{0:T(256)S(1)} %get-tuple-element.31) | copy-start | bytes 2308
  12.6 10.1 collective-permute-start.1
  17.1 11.5 %collective-permute-start = (bf16[64,8,128]{2,0,1:T(8,128)(2,1)S(1)}, bf16[64,8,128]{2,0,1:T(8,128)(2,1)S(1)}, u32[]{:S(2)}, u32[]{:S(2)}) collective-permute-start(bf16[64,8,128]{2,0,1:T(8,128)(2,1)S(1)} %slice.343), channel_id=1, source_target_pairs={{0,4},{4,8},{8,12},{12,16},{16,20},{20,24},{24,28},{28,32},{32,36}... | collective-permute-start | bytes 393224 | tf_op jit(solution)/shard_map/ppermute | solution.py:18
  22.8 5.7 copy-start.35
  23.4 8.4 copy-start.33
  27.6 1.1 copy-start.7
  28.7 42.3 %copy-start.20 = (bf16[256,8,128]{2,0,1:T(8,128)(2,1)}, bf16[256,8,128]{2,0,1:T(8,128)(2,1)S(1)}, u32[]{:S(2)}) copy-start(bf16[256,8,128]{2,0,1:T(8,128)(2,1)S(1)} %constant_dynamic-update-slice_fusion) | copy-start | bytes 1572868
  29.3 1.0 copy-start.5
  31.9 643.8 %all-gather.12.cloned.1.call-start = ((), (), s32[]{:S(2)}) async-start(), calls=%async_computation.2 | async-start | bytes 4718592 | tf_op jit(solution)/shard_map/all_gather | solution.py:32
  70.2 612.7 %all-gather.10.cloned.1.call-start = ((), (), s32[]{:S(2)}) async-start(), calls=%async_computation.1 | async-start | bytes 12976128 | tf_op jit(solution)/shard_map/all_gather | solution.py:85
  78.6 8.9 copy-start.39
  78.6 402.4 %copy-start.38 = (u32[256]{0:T(256)S(1)}, u32[256]{0:T(256)}, u32[]{:S(2)}) copy-start(u32[256]{0:T(256)} %constant.88) | copy-start | bytes 3076
  78.6 541.7 %copy-start.37 = (s32[192]{0:T(256)S(1)}, s32[192]{0:T(256)}, u32[]{:S(2)}) copy-start(s32[192]{0:T(256)} %param.8) | copy-start | bytes 2308
  78.6 541.7 %copy-start.6 = (f32[8,128,128]{2,1,0:T(8,128)S(1)}, f32[8,128,128]{2,1,0:T(8,128)}, u32[]{:S(2)}) copy-start(f32[8,128,128]{2,1,0:T(8,128)} %param.9) | copy-start | bytes 1572868
  78.6 640.9 %all-to-all-start = ((bf16[32,192,8,128]{3,1,2,0:T(8,128)(2,1)}), bf16[32,192,8,128]{3,1,2,0:T(8,128)(2,1)}, u32[]{:S(2)}, u32[]{:S(2)}) async-start(bf16[32,192,8,128]{3,1,2,0:T(8,128)(2,1)} %stack.2), calls=%async_computation | async-start | bytes 25165824 | tf_op jit(solution)/shard_map/all_to_all | solution.py:90
  87.5 536.5 %copy-start.32 = (f32[192]{0:T(256)S(1)}, f32[192]{0:T(256)}, u32[]{:S(2)}) copy-start(f32[192]{0:T(256)} %copy-done.31) | copy-start | bytes 2308
  87.5 537.5 %copy-start.36 = (f32[256]{0:T(256)S(1)}, f32[256]{0:T(256)}, u32[]{:S(2)}) copy-start(f32[256]{0:T(256)} %copy-done.35) | copy-start | bytes 3076
  87.5 537.6 %copy-start.34 = (f32[192]{0:T(256)S(1)}, f32[192]{0:T(256)}, u32[]{:S(2)}) copy-start(f32[192]{0:T(256)} %copy-done.33) | copy-start | bytes 2308
  87.5 703.6 %all-gather.18.cloned.1.call-start = ((), (), s32[]{:S(2)}) async-start(), calls=%async_computation.7 | async-start | bytes 2621440 | tf_op jit(solution)/shard_map/all_gather | solution.py:32
  622.1 0.9 copy-start.11
  668.8 1.0 copy-start.15
  669.7 0.8 copy-start.17
  669.8 2.8 copy-start.1
  669.8 2.8 copy-start.2
  679.4 0.8 copy-start.3
  731.3 21.6 %copy-start.21 = (bf16[256,8,128]{2,0,1:T(8,128)(2,1)S(1)}, bf16[256,8,128]{2,0,1:T(8,128)(2,1)}, u32[]{:S(2)}) copy-start(bf16[256,8,128]{2,0,1:T(8,128)(2,1)} %copy-done.20) | copy-start | bytes 1572868
  731.3 21.6 %copy-start.25 = (f32[8,192,256]{2,1,0:T(8,128)S(1)}, f32[8,192,256]{2,1,0:T(8,128)}, u32[]{:S(2)}) copy-start(f32[8,192,256]{2,1,0:T(8,128)} %get-tuple-element.69) | copy-start | bytes 4718596
  731.3 21.6 %copy-start.26 = (f32[8,128,192]{1,2,0:T(8,128)S(1)}, f32[8,128,192]{1,2,0:T(8,128)}, u32[]{:S(2)}) copy-start(f32[8,128,192]{1,2,0:T(8,128)} %convolution_multiply_fusion.1) | copy-start | bytes 2359300
  752.8 3.7 copy-start.27
  759.1 118.2 %all-gather.14.cloned.1.call-start = ((), (), s32[]{:S(2)}) async-start(), calls=%async_computation.3 | async-start | bytes 4718592 | tf_op jit(solution)/shard_map/all_gather | solution.py:32
  793.6 160.9 %all-reduce.12.cloned.1.call-start = ((), (), s32[]{:S(2)}) async-start(), calls=%async_computation.4 | async-start | bytes 1048576 | tf_op jit(solution)/shard_map/psum | solution.py:43
  829.7 6.1 copy-start.12
  829.7 6.1 copy-start.14
  832.8 4.5 copy-start.16
  832.8 4.5 copy-start.18
  875.3 2.0 copy-start.22
  875.3 2.0 copy-start.23
  877.2 4.3 copy-start.8
  877.2 4.3 copy-start.10
  881.5 1.0 copy-start.30
  881.7 93.0 %copy-start.29 = (bf16[192,8,128]{2,0,1:T(8,128)(2,1)S(1)}, bf16[192,8,128]{2,0,1:T(8,128)(2,1)}, u32[]{:S(2)}) copy-start(bf16[192,8,128]{2,0,1:T(8,128)(2,1)} %get-tuple-element.22) | copy-start | bytes 1179652
  881.7 94.0 %copy-start.28 = (bf16[192,8,128]{2,0,1:T(8,128)(2,1)S(1)}, bf16[192,8,128]{2,0,1:T(8,128)(2,1)}, u32[]{:S(2)}) copy-start(bf16[192,8,128]{2,0,1:T(8,128)(2,1)} %get-tuple-element.25) | copy-start | bytes 1179652
  883.3 120.0 %all-reduce.14.cloned.1.call-start = ((), (), s32[]{:S(2)}) async-start(), calls=%async_computation.5 | async-start | bytes 1048576 | tf_op jit(solution)/shard_map/psum | solution.py:43
  (3 other events, 2.4 us)
Sparse Core Ops, SparseCore 0:
  32.0 35.6 all-gather.15
  70.3 134.1 all-gather.11
  207.6 271.7 all-gather.9
  759.2 31.8 all-gather.17
  793.7 55.0 all-gather.13
  883.4 71.0 all-reduce.11
  956.8 46.4 all-reduce.13
